TPU v7x, 128 devices: a whole 4x4x4 slice. The times are simulated.
128 devices in a mesh: section: 8 (over y, z_lo), dp: 16 (over x, z_hi, core).
Axes of the slice: x: 4, y: 4, z: 4 (z_hi: 2, z_lo: 2; z = z_hi * 2 + z_lo), core: 2. Of those that a mesh axis runs over, the one named last changes fastest.
Arguments:
- enter_a: bfloat16 [8, 2048, 7168], P('section', 'dp'), may hold values from -6 to 6
- enter_b: bfloat16 [8, 2048, 7168], P('section', 'dp'), may hold values from -6 to 6
- cotan_a: bfloat16 [8, 2048, 7168], P('section', 'dp'), may hold values from -6 to 6
- cotan_b: bfloat16 [8, 2048, 7168], P('section', 'dp'), may hold values from -6 to 6
- saved_a: bfloat16 [2, 8, 2048, 7168], P(None, 'section', 'dp'), may hold values from -6 to 6
- saved_b: bfloat16 [2, 8, 2048, 7168], P(None, 'section', 'dp'), may hold values from -6 to 6
- norm_gain: float32 [8, 7168], P('section'), may hold values from 0.1 to 1.9
- w_down: bfloat16 [8, 7168, 256], P('section', 'dp'), may hold values from -0.0625 to 0.0625
- latent_gain: float32 [8, 256], P('section'), may hold values from 0.1 to 1.9
- w_up: bfloat16 [8, 256, 7168], P('section', None, 'dp'), may hold values from -0.375 to 0.375
Outputs:
- out_a: bfloat16 [8, 2048, 7168], P('section', 'dp')
- out_b: bfloat16 [8, 2048, 7168], P('section', 'dp')
- back_a: bfloat16 [8, 2048, 7168], P('section', 'dp')
- back_b: bfloat16 [8, 2048, 7168], P('section', 'dp')
- grad_norm_gain: float32 [8, 7168], P('section', 'dp')
- grad_down: float32 [8, 7168, 256], P('section', 'dp')
- grad_latent_gain: float32 [8, 256], P('section', 'dp')
- grad_up: float32 [8, 256, 7168], P('section', None, 'dp')
All inputs are finite; a program needn't handle non-finite values.
Results may differ from a plain program's by a relative error of at most 0.035.
Values may be sent and summed in bfloat16 or wider, within the bound.
No kernel may reach another device: no remote copies, remote signals or barrier semaphores. Data moves between devices by JAX's collectives and lax.ppermute only.
A program may use at most 192 MiB of HBM per device.

v0:
```python
import jax
import jax.numpy as jnp
from jax import lax
from jax.sharding import PartitionSpec as P

TICKS = 2


def swapped(value, axis, distance):
    return lax.ppermute(value, axis, [(i, i ^ 1 << distance) for i in range(lax.axis_size(axis))])


def from_behind(block, axis, distance):
    devices = range(lax.axis_size(axis))
    route = [(i - distance, i) for i in devices if i - distance in devices]
    return lax.ppermute(block, axis, route)


def shortened(value):

    def short(part):
        return part.astype(jnp.bfloat16) if part.dtype == jnp.float32 else part

    return jax.tree.map(short, value)


def layer(x, norm_gain, w_down, latent_gain, w_up):
    xf = x.astype(jnp.float32)
    normed = (xf * lax.rsqrt(jnp.mean(xf * xf, axis=-1, keepdims=True) + 1e-06) * norm_gain).astype(
        jnp.bfloat16
    )
    latent = jnp.dot(normed, w_down, preferred_element_type=jnp.float32)
    scaled = (
        latent * lax.rsqrt(jnp.mean(latent * latent, axis=-1, keepdims=True) + 1e-06) * latent_gain
    ).astype(jnp.bfloat16)
    return (xf + jnp.dot(scaled, w_up, preferred_element_type=jnp.float32)).astype(jnp.bfloat16)


def layer_grads(x, cotangent, weights):
    _, pull = jax.vjp(layer, x, *weights)
    return pull(cotangent)


def body(
    enter_a, enter_b, cotan_a, cotan_b, saved_a, saved_b, norm_gain, w_down, latent_gain, w_up
):
    section_count = lax.axis_size("section")
    section_bits = section_count.bit_length() - 1
    moved = (norm_gain, w_down, latent_gain, w_up)
    for bit in range(section_bits):
        moved = (
            swapped(moved[0].astype(jnp.bfloat16), "section", bit).astype(jnp.float32),
            swapped(moved[1], "section", bit),
            swapped(moved[2].astype(jnp.bfloat16), "section", bit).astype(jnp.float32),
            swapped(moved[3], "section", bit),
        )
    mirror_small = tuple((v[0] for v in moved))
    full = (
        lax.all_gather(w_down[0], "dp", axis=0, tiled=True),
        lax.all_gather(w_up[0], "dp", axis=1, tiled=True),
        lax.all_gather(mirror_small[1], "dp", axis=0, tiled=True),
        lax.all_gather(mirror_small[3], "dp", axis=1, tiled=True),
    )
    own_weights = (norm_gain[0], full[0], latent_gain[0], full[1])
    mirror_weights = (mirror_small[0], full[2], mirror_small[2], full[3])
    accum_own = tuple((jnp.zeros(v.shape, jnp.float32) for v in own_weights))
    accum_mirror = tuple((jnp.zeros(v.shape, jnp.float32) for v in mirror_weights))
    state_a = enter_a[0]
    state_b = enter_b[0]
    grad_a = cotan_a[0]
    grad_b = cotan_b[0]
    for tick in range(TICKS):
        out_a = layer(state_a, *own_weights)
        out_b = layer(state_b, *mirror_weights)
        result_a = layer_grads(saved_a[tick, 0], grad_a, own_weights)
        result_b = layer_grads(saved_b[tick, 0], grad_b, mirror_weights)
        back_a = result_a[0]
        back_b = result_b[0]
        accum_own = tuple((p + q.astype(jnp.float32) for p, q in zip(accum_own, result_a[1:])))
        accum_mirror = tuple(
            (p + q.astype(jnp.float32) for p, q in zip(accum_mirror, result_b[1:]))
        )
        if tick < TICKS - 1:
            state_a = from_behind(out_a, "section", 1)
            state_b = from_behind(out_b, "section", -1)
            grad_a = from_behind(back_a, "section", -1)
            grad_b = from_behind(back_b, "section", 1)
    part_own = tuple((v.astype(jnp.bfloat16) for v in accum_own))
    part_mirror = tuple((v.astype(jnp.bfloat16) for v in accum_mirror))
    paired = tuple((jnp.stack([p, q]) for p, q in zip(part_own, part_mirror)))
    sums = (
        lax.psum_scatter(paired[0], "dp", scatter_dimension=1, tiled=True).astype(jnp.float32),
        lax.psum_scatter(paired[1], "dp", scatter_dimension=1, tiled=True).astype(jnp.float32),
        lax.psum_scatter(paired[2], "dp", scatter_dimension=1, tiled=True).astype(jnp.float32),
        lax.psum_scatter(paired[3], "dp", scatter_dimension=2, tiled=True).astype(jnp.float32),
    )
    mine = tuple((v[0] for v in sums))
    theirs = tuple((v[1] for v in sums))
    arrived = theirs
    for bit in range(section_bits):
        arrived = swapped(
            (
                shortened(arrived[0]),
                shortened(arrived[1]),
                shortened(arrived[2]),
                shortened(arrived[3]),
            ),
            "section",
            bit,
        )
    totals = tuple((p + q for p, q in zip(mine, arrived)))
    return (
        out_a[None],
        out_b[None],
        back_a[None],
        back_b[None],
        totals[0][None],
        totals[1][None],
        totals[2][None],
        totals[3][None],
    )


def solution(mesh):
    placed = (
        P("section", "dp", None),
        P("section", "dp", None),
        P("section", "dp", None),
        P("section", "dp", None),
        P(None, "section", "dp", None),
        P(None, "section", "dp", None),
        P("section", None),
        P("section", "dp", None),
        P("section", None),
        P("section", None, "dp"),
    )
    return jax.shard_map(
        body,
        mesh=mesh,
        in_specs=placed,
        out_specs=(
            P("section", "dp", None),
            P("section", "dp", None),
            P("section", "dp", None),
            P("section", "dp", None),
            P("section", "dp"),
            P("section", "dp", None),
            P("section", "dp"),
            P("section", None, "dp"),
        ),
        check_vma=False,
    )
```

profile of v0, /device:TPU:0, one launch (start us, length us, event | category | flops | bytes accessed | tf_op | source)
XLA Modules:
  0.0 882.6 jit_solution(12329885674693998641)
XLA Ops:
  10.8 5.8 collective-permute-done.4
  18.2 5.2 collective-permute-done.5
  23.4 3.1 collective-permute-start.6
  26.5 4.4 collective-permute-done.6
  33.2 4.8 collective-permute-done.10
  39.4 4.6 collective-permute-done.11
  44.1 4.3 collective-permute-start.12
  48.4 4.0 collective-permute-done.12
  64.3 3.9 collective-permute-start.9
  70.5 3.0 collective-permute-done.3
  73.6 3.5 multiply_reduce_fusion.11
  77.1 45.5 %all-gather.11.cloned.1.call-done = bf16[1,256,7168]{1,2,0:T(8,128)(2,1)} async-done(((bf16[1,256,448]{1,2,0:T(8,128)(2,1)}), bf16[1,256,7168]{1,2,0:T(8,128)(2,1)}) %all-gather.11.cloned.1.call-update) | async-done | bytes 3670032 | tf_op jit(solution)/shard_map/all_gather | solution.py:60
  122.7 2.9 multiply_reduce_fusion.3
  125.8 3.8 fusion.45
  134.6 4.2 fusion.8
  138.8 78.3 %all-gather.13.cloned.1.call-done = bf16[1,7168,256]{2,1,0:T(8,128)(2,1)} async-done(((bf16[1,448,256]{2,1,0:T(8,128)(2,1)}), bf16[1,7168,256]{2,1,0:T(8,128)(2,1)}) %all-gather.13.cloned.1.call-update) | async-done | bytes 3670032 | tf_op jit(solution)/shard_map/all_gather | solution.py:61
  217.1 3.5 multiply_reduce_fusion.7
  220.6 52.1 %all-gather.15.cloned.1.call-done = bf16[1,256,7168]{1,2,0:T(8,128)(2,1)} async-done(((bf16[1,256,448]{1,2,0:T(8,128)(2,1)}), bf16[1,256,7168]{1,2,0:T(8,128)(2,1)}) %all-gather.15.cloned.1.call-update) | async-done | bytes 3670032 | tf_op jit(solution)/shard_map/all_gather | solution.py:62
  272.7 2.9 multiply_reduce_fusion.1
  275.9 3.8 fusion.41
  286.9 2.8 fusion.17
  289.7 33.4 %collective-permute-done.15 = bf16[128,7168]{1,0:T(8,128)(2,1)S(1)} collective-permute-done((bf16[128,7168]{1,0:T(8,128)(2,1)S(1)}, bf16[128,7168]{1,0:T(8,128)(2,1)S(1)}, u32[]{:S(2)}, u32[]{:S(2)}) %collective-permute-start.15) | collective-permute-done | bytes 1835040 | tf_op jit(solution)/shard_map/ppermute | solution.py:16
  325.5 3.7 pad_maximum_fusion.1
  329.2 18.5 %copy.21 = bf16[2,256,7168]{1,0,2:T(2,128)(2,1)} copy(bf16[2,256,7168]{2,1,0:T(8,128)(2,1)} %pad_maximum_fusion.1) | data formatting | bytes 14680064 | tf_op jit(solution)/shard_map/stack | solution.py:90
  348.0 3.5 multiply_reduce_fusion.2
  351.6 5.4 fusion.43
  358.4 3.3 fusion.19
  364.5 3.4 fusion.39
  369.8 2.9 fusion.7
  372.7 3.2 fusion.18
  376.0 6.8 pad_maximum_fusion
  385.0 3.5 multiply_reduce_fusion.15
  391.9 5.8 collective-permute-start
  400.9 3.6 multiply_reduce_fusion.13
  409.0 103.3 %collective-permute-done = bf16[128,7168]{1,0:T(8,128)(2,1)} collective-permute-done((bf16[128,7168]{1,0:T(8,128)(2,1)}, bf16[128,7168]{1,0:T(8,128)(2,1)}, u32[]{:S(2)}, u32[]{:S(2)}) %collective-permute-start) | collective-permute-done | bytes 1835040 | tf_op jit(solution)/shard_map/ppermute | solution.py:16
  516.9 4.2 fusion.29
  521.1 3.9 fusion.105
  527.9 3.4 multiply_reduce_fusion.12
  531.3 5.0 fusion.104
  536.3 68.5 %all-reduce.3.cloned.1.call-done = bf16[2,256,7168]{1,0,2:T(2,128)(2,1)} async-done(((bf16[2,256,7168]{1,0,2:T(2,128)(2,1)}), bf16[2,256,7168]{1,0,2:T(2,128)(2,1)}) %all-reduce.3.cloned.1.call-update) | async-done | bytes 7340048
  606.9 73.6 %reduce-scatter.10.cloned.1.call-done = bf16[448,2]{1,0:T(8,128)(2,1)} async-done(((bf16[7168,2]{1,0:T(8,128)(2,1)}), bf16[448,2]{1,0:T(8,128)(2,1)}) %reduce-scatter.10.cloned.1.call-update) | async-done | bytes 1808
  684.0 94.5 %reduce-scatter.8.cloned.1.call-done = bf16[2,448,256]{2,1,0:T(8,128)(2,1)} async-done(((bf16[2,7168,256]{2,1,0:T(8,128)(2,1)}), bf16[2,448,256]{2,1,0:T(8,128)(2,1)}) %reduce-scatter.8.cloned.1.call-update) | async-done | bytes 458768 | tf_op jit(solution)/shard_map/reduce_scatter | solution.py:93
  780.4 5.2 fusion.28
  787.1 55.9 %reduce-scatter.12.cloned.1.call-done = bf16[16,2]{1,0:T(8,128)(2,1)} async-done(((bf16[256,2]{1,0:T(8,128)(2,1)}), bf16[16,2]{1,0:T(8,128)(2,1)}) %reduce-scatter.12.cloned.1.call-update) | async-done | bytes 80
  851.1 3.0 collective-permute-start.24
  854.7 3.0 collective-permute-start.27
  859.8 7.4 collective-permute-done.20
  869.4 5.3 collective-permute-done.21
  (185 shorter events, 87.4 us)
Async XLA Ops:
  7.2 66.4 %copy-start.17 = (f32[1,7168]{1,0:T(1,128)S(1)}, f32[1,7168]{1,0:T(1,128)}, u32[]{:S(2)}) copy-start(f32[1,7168]{1,0:T(1,128)} %param.16) | copy-start | bytes 86020
  7.2 66.4 %all-gather.9.cloned.1.call-start = ((), (), s32[]{:S(2)}) async-start(), calls=%async_computation.4 | async-start | bytes 3899392 | tf_op jit(solution)/shard_map/all_gather | solution.py:59
  7.9 114.7 %all-gather.11.cloned.1.call-start = ((), (), s32[]{:S(2)}) async-start(), calls=%async_computation.5 | async-start | bytes 3899392 | tf_op jit(solution)/shard_map/all_gather | solution.py:60
  8.7 208.4 %all-gather.13.cloned.1.call-start = ((), (), s32[]{:S(2)}) async-start(), calls=%async_computation.6 | async-start | bytes 3899392 | tf_op jit(solution)/shard_map/all_gather | solution.py:61
  8.7 7.9 collective-permute-start.4
  16.6 6.8 collective-permute-start.5
  23.4 7.5 collective-permute-start.6
  31.6 241.1 %all-gather.15.cloned.1.call-start = ((), (), s32[]{:S(2)}) async-start(), calls=%async_computation.7 | async-start | bytes 3899392 | tf_op jit(solution)/shard_map/all_gather | solution.py:62
  31.7 6.3 collective-permute-start.10
  38.0 6.1 collective-permute-start.11
  44.1 8.3 collective-permute-start.12
  53.1 551.8 %all-reduce.3.cloned.1.call-start = ((), (), s32[]{:S(2)}) async-start(), calls=%async_computation.10 | async-start | bytes 14680064
  53.9 8.5 collective-permute-start.1
  56.5 4.1 collective-permute-start.7
  60.6 3.6 collective-permute-start.8
  62.4 5.8 collective-permute-start.2
  64.3 6.2 collective-permute-start.9
  68.2 5.4 collective-permute-start.3
  73.6 49.0 %copy-start.10 = (bf16[1,128,7168]{2,1,0:T(8,128)(2,1)S(1)}, bf16[1,128,7168]{2,1,0:T(8,128)(2,1)}, u32[]{:S(2)}) copy-start(bf16[1,128,7168]{2,1,0:T(8,128)(2,1)} %param.12) | copy-start | bytes 5505028
  73.6 49.0 %copy-start.21 = (f32[1,256]{1,0:T(1,128)S(1)}, f32[1,256]{1,0:T(1,128)}, u32[]{:S(2)}) copy-start(f32[1,256]{1,0:T(1,128)} %param.18) | copy-start | bytes 3076
  129.6 4.3 copy-start.22
  132.0 153.6 %collective-permute-start.14 = (bf16[128,7168]{1,0:T(8,128)(2,1)}, bf16[128,7168]{1,0:T(8,128)(2,1)}, u32[]{:S(2)}, u32[]{:S(2)}) collective-permute-start(bf16[128,7168]{1,0:T(8,128)(2,1)} %fusion.52), channel_id=1, source_target_pairs={{16,0},{32,16},{48,32},{64,48},{80,64},{96,80},{112,96},{17,1},{33... | collective-permute-start | bytes 5505032 | tf_op jit(solution)/shard_map/ppermute | solution.py:16
  217.1 55.7 %copy-start.11 = (bf16[1,128,7168]{2,1,0:T(8,128)(2,1)S(1)}, bf16[1,128,7168]{2,1,0:T(8,128)(2,1)}, u32[]{:S(2)}) copy-start(bf16[1,128,7168]{2,1,0:T(8,128)(2,1)} %param.13) | copy-start | bytes 5505028
  280.9 42.2 %collective-permute-start.15 = (bf16[128,7168]{1,0:T(8,128)(2,1)S(1)}, bf16[128,7168]{1,0:T(8,128)(2,1)S(1)}, u32[]{:S(2)}, u32[]{:S(2)}) collective-permute-start(bf16[128,7168]{1,0:T(8,128)(2,1)S(1)} %fusion.54), channel_id=1, source_target_pairs={{0,16},{16,32},{32,48},{48,64},{64,80},{80,96},{96,112},{1,17},{17... | collective-permute-start | bytes 5505032 | tf_op jit(solution)/shard_map/ppermute | solution.py:16
  347.7 332.8 %reduce-scatter.10.cloned.1.call-start = ((), (), s32[]{:S(2)}) async-start(), calls=%async_computation.8 | async-start | bytes 1949696
  358.4 5.0 copy-start.25
  375.9 402.6 %reduce-scatter.8.cloned.1.call-start = ((), (), s32[]{:S(2)}) async-start(), calls=%async_computation.3 | async-start | bytes 7798784 | tf_op jit(solution)/shard_map/reduce_scatter | solution.py:93
  382.8 460.2 %reduce-scatter.12.cloned.1.call-start = ((), (), s32[]{:S(2)}) async-start(), calls=%async_computation.9 | async-start | bytes 69632
  385.0 4.3 copy-start.14
  389.3 8.3 copy-start.26
  391.9 120.5 %collective-permute-start = (bf16[128,7168]{1,0:T(8,128)(2,1)}, bf16[128,7168]{1,0:T(8,128)(2,1)}, u32[]{:S(2)}, u32[]{:S(2)}) collective-permute-start(bf16[128,7168]{1,0:T(8,128)(2,1)} %fusion.20), channel_id=1, source_target_pairs={{0,16},{16,32},{32,48},{48,64},{64,80},{80,96},{96,112},{1,17},{17... | collective-permute-start | bytes 5505032 | tf_op jit(solution)/shard_map/ppermute | solution.py:16
  400.9 4.3 copy-start.15
  405.2 109.2 %copy-start.23 = (bf16[1,7168,256]{2,1,0:T(8,128)(2,1)S(1)}, bf16[1,7168,256]{2,1,0:T(8,128)(2,1)}, u32[]{:S(2)}) copy-start(bf16[1,7168,256]{2,1,0:T(8,128)(2,1)} %all-gather.9.cloned.1.call-done) | copy-start | bytes 11010052
  407.7 118.1 %collective-permute-start.13 = (bf16[128,7168]{1,0:T(8,128)(2,1)}, bf16[128,7168]{1,0:T(8,128)(2,1)}, u32[]{:S(2)}, u32[]{:S(2)}) collective-permute-start(bf16[128,7168]{1,0:T(8,128)(2,1)} %fusion.22), channel_id=1, source_target_pairs={{16,0},{32,16},{48,32},{64,48},{80,64},{96,80},{112,96},{17,1},{33... | collective-permute-start | bytes 5505032 | tf_op jit(solution)/shard_map/ppermute | solution.py:16
  516.9 4.2 copy-start.16
  606.8 75.7 %collective-permute-start.25 = (bf16[256,448]{0,1:T(8,128)(2,1)S(1)}, bf16[256,448]{0,1:T(8,128)(2,1)S(1)}, u32[]{:S(2)}, u32[]{:S(2)}) collective-permute-start(bf16[256,448]{0,1:T(8,128)(2,1)S(1)} %bitcast.261), channel_id=1, source_target_pairs={{0,16},{16,0},{32,48},{48,32},{64,80},{80,64},{96,112},{112,96},{1... | collective-permute-start | bytes 688136 | tf_op jit(solution)/shard_map/ppermute | solution.py:10
  681.7 104.0 %collective-permute-start.16 = (bf16[448]{0:T(512)(128)(2,1)S(1)}, bf16[448]{0:T(512)(128)(2,1)S(1)}, u32[]{:S(2)}, u32[]{:S(2)}) collective-permute-start(bf16[448]{0:T(512)(128)(2,1)S(1)} %get-tuple-element.36), channel_id=1, source_target_pairs={{0,16},{16,0},{32,48},{48,32},{64,80},{80,64},{96,112},{112,96},{1... | collective-permute-start | bytes 2696 | tf_op jit(solution)/shard_map/ppermute | solution.py:10
  682.5 172.1 %collective-permute-start.26 = (bf16[256,448]{0,1:T(8,128)(2,1)S(1)}, bf16[256,448]{0,1:T(8,128)(2,1)S(1)}, u32[]{:S(2)}, u32[]{:S(2)}) collective-permute-start(bf16[256,448]{0,1:T(8,128)(2,1)S(1)} %collective-permute-done.25), channel_id=1, source_target_pairs={{0,32},{16,48},{32,0},{48,16},{64,96},{80,112},{96,64},{112,80},{1... | collective-permute-start | bytes 688136 | tf_op jit(solution)/shard_map/ppermute | solution.py:10
  779.5 78.2 %collective-permute-start.19 = (bf16[448,256]{1,0:T(8,128)(2,1)S(1)}, bf16[448,256]{1,0:T(8,128)(2,1)S(1)}, u32[]{:S(2)}, u32[]{:S(2)}) collective-permute-start(bf16[448,256]{1,0:T(8,128)(2,1)S(1)} %slice_bitcast_fusion), channel_id=1, source_target_pairs={{0,16},{16,0},{32,48},{48,32},{64,80},{80,64},{96,112},{112,96},{1... | collective-permute-start | bytes 688136 | tf_op jit(solution)/shard_map/ppermute | solution.py:10
  780.4 94.2 %copy-start.18 = (bf16[2,448,256]{2,1,0:T(8,128)(2,1)S(1)}, bf16[2,448,256]{2,1,0:T(8,128)(2,1)}, u32[]{:S(2)}) copy-start(bf16[2,448,256]{2,1,0:T(8,128)(2,1)} %reduce-scatter.8.cloned.1.call-done) | copy-start | bytes 1376260
  785.6 68.5 %collective-permute-start.17 = (bf16[448]{0:T(512)(128)(2,1)S(1)}, bf16[448]{0:T(512)(128)(2,1)S(1)}, u32[]{:S(2)}, u32[]{:S(2)}) collective-permute-start(bf16[448]{0:T(512)(128)(2,1)S(1)} %collective-permute-done.16), channel_id=1, source_target_pairs={{0,32},{16,48},{32,0},{48,16},{64,96},{80,112},{96,64},{112,80},{1... | collective-permute-start | bytes 2696 | tf_op jit(solution)/shard_map/ppermute | solution.py:10
  844.0 3.5 collective-permute-start.22
  847.6 3.5 collective-permute-start.23
  851.1 7.1 collective-permute-start.24
  854.1 5.1 collective-permute-start.18
  854.7 13.9 %collective-permute-start.27 = (bf16[256,448]{0,1:T(8,128)(2,1)S(1)}, bf16[256,448]{0,1:T(8,128)(2,1)S(1)}, u32[]{:S(2)}, u32[]{:S(2)}) collective-permute-start(bf16[256,448]{0,1:T(8,128)(2,1)S(1)} %collective-permute-done.26), channel_id=1, source_target_pairs={{0,64},{16,80},{32,96},{48,112},{64,0},{80,16},{96,32},{112,48},{1... | collective-permute-start | bytes 688136 | tf_op jit(solution)/shard_map/ppermute | solution.py:10
  857.6 9.5 %collective-permute-start.20 = (bf16[448,256]{1,0:T(8,128)(2,1)S(1)}, bf16[448,256]{1,0:T(8,128)(2,1)S(1)}, u32[]{:S(2)}, u32[]{:S(2)}) collective-permute-start(bf16[448,256]{1,0:T(8,128)(2,1)S(1)} %collective-permute-done.19), channel_id=1, source_target_pairs={{0,32},{16,48},{32,0},{48,16},{64,96},{80,112},{96,64},{112,80},{1... | collective-permute-start | bytes 688136 | tf_op jit(solution)/shard_map/ppermute | solution.py:10
  867.2 7.5 collective-permute-start.21
  (17 other events, 48.0 us)
Sparse Core Ops, SparseCore 0:
  10.4 56.9 all-gather.8
  69.8 52.7 all-gather.10
  125.6 91.4 all-gather.12
  219.9 52.7 all-gather.14
  347.9 256.9 all-reduce.2
  608.6 71.8 reduce-scatter.9
  685.3 93.1 reduce-scatter.7
  782.6 60.3 reduce-scatter.11
where the time goes:
time: 890 us; the launch traced here: 883 us
  waiting for transfers between devices  658 us (74%)
  matrix products  82.5 us (9%)
  starting transfers between devices  52.4 us (6%)
  other arithmetic  40.5 us (5%)
  local copies, waits for them, and re-layouts  33.8 us (4%)
  between operations  15.5 us (2%)
    unnamed x11, waiting for transfers between devices  199 us
    ppermute x4, waiting for transfers between devices, from_behind(): return lax.ppermute(block, axis, route)  137 us
    reduce_scatter x1, waiting for transfers between devices, body(): lax.psum_scatter(paired[1], 'dp', scatter_dimension=1, tiled=True)  94.5 us
    all_gather x1, waiting for transfers between devices, body(): lax.all_gather(mirror_small[1], 'dp', axis=0, tiled=True)  78.3 us
    all_gather x1, waiting for transfers between devices, body(): lax.all_gather(mirror_small[3], 'dp', axis=1, tiled=True)  52.1 us
    ppermute x24, waiting for transfers between devices, swapped(): lax.ppermute(value, axis, [(i, i ^ 1 << distance) for i in range(lax.axis...  51.3 us
    dot_general x16, matrix products, layer(): latent = jnp.dot(normed, w_down, preferred_element_type=jnp.float32)  48.5 us
    all_gather x1, waiting for transfers between devices, body(): lax.all_gather(w_up[0], 'dp', axis=1, tiled=True)  45.5 us
  transfers between devices with their start and end apart: 36, of which 22 were waited for; matrix products, arithmetic and copies ran while one was open for 14% of the time, Pallas kernels for 0%

commit v1 on v0

--- a/solution.py
+++ b/solution.py
@@ -55,11 +55,14 @@
             swapped(moved[3], "section", bit),
         )
     mirror_small = tuple((v[0] for v in moved))
+    shapes_watch = lambda vector: jnp.concatenate(
+        jax.lax.all_to_all(jnp.stack([vector] * jax.lax.axis_size("dp"), axis=0), "dp", 0, 0), 1
+    )
     full = (
         lax.all_gather(w_down[0], "dp", axis=0, tiled=True),
         lax.all_gather(w_up[0], "dp", axis=1, tiled=True),
         lax.all_gather(mirror_small[1], "dp", axis=0, tiled=True),
-        lax.all_gather(mirror_small[3], "dp", axis=1, tiled=True),
+        shapes_watch(mirror_small[3]),
     )
     own_weights = (norm_gain[0], full[0], latent_gain[0], full[1])
     mirror_weights = (mirror_small[0], full[2], mirror_small[2], full[3])

time: 890 us -> 857 us (0.963)
  waiting for transfers between devices: 658 us -> 616 us
    all_gather x1 -> x0, waiting for transfers between devices: 52.1 us -> none  [body(): lax.all_gather(mirror_small[3], 'dp', axis=1, tiled=True)]
    all_gather x1, waiting for transfers between devices: 45.5 us -> 69 us  [body(): lax.all_gather(w_up[0], 'dp', axis=1, tiled=True)]
    ppermute x24, waiting for transfers between devices: 51.3 us -> 36 us  [swapped(): lax.ppermute(value, axis, [(i, i ^ 1 << distance) for i in range(lax.axis...]
    unnamed x11 -> x10, waiting for transfers between devices: 199 us -> 200 us
  transfers between devices with their start and end apart: 36 -> 36, of which waited for: 22 -> 20; matrix products, arithmetic and copies ran while one was open for 14% -> 15% of each run, Pallas kernels for 0% -> 0%
where the time goes in v1:
time: 857 us; the launch traced here: 850 us
  waiting for transfers between devices  616 us (72%)
  matrix products  86.7 us (10%)
  starting transfers between devices  58 us (7%)
  other arithmetic  40.5 us (5%)
  local copies, waits for them, and re-layouts  32.9 us (4%)
  between operations  15.5 us (2%)
    unnamed x10, waiting for transfers between devices  200 us
    ppermute x4, waiting for transfers between devices, from_behind(): return lax.ppermute(block, axis, route)  135 us
    reduce_scatter x1, waiting for transfers between devices, body(): lax.psum_scatter(paired[1], 'dp', scatter_dimension=1, tiled=True)  94.4 us
    all_gather x1, waiting for transfers between devices, body(): lax.all_gather(mirror_small[1], 'dp', axis=0, tiled=True)  80.2 us
    all_gather x1, waiting for transfers between devices, body(): lax.all_gather(w_up[0], 'dp', axis=1, tiled=True)  69 us
    dot_general x16, matrix products, layer(): latent = jnp.dot(normed, w_down, preferred_element_type=jnp.float32)  48.5 us
    dot_general x12, matrix products, layer(): jnp.dot(scaled, w_up, preferred_element_type=jnp.float32)  38.3 us
    ppermute x24, starting transfers between devices, swapped(): lax.ppermute(value, axis, [(i, i ^ 1 << distance) for i in range(lax.axis...  37.8 us
  transfers between devices with their start and end apart: 36, of which 20 were waited for; matrix products, arithmetic and copies ran while one was open for 15% of the time, Pallas kernels for 0%

profile of v1, /device:TPU:0, one launch (start us, length us, event | category | flops | bytes accessed | tf_op | source)
XLA Modules:
  0.0 849.6 jit_solution(6872794126661629561)
XLA Ops:
  10.8 5.8 collective-permute-done.4
  18.2 5.2 collective-permute-done.5
  23.4 3.1 collective-permute-start.6
  26.5 4.4 collective-permute-done.6
  45.3 4.3 collective-permute-start.12
  49.6 3.4 collective-permute-start.3
  57.3 8.1 all-to-all-start
  67.1 3.5 multiply_reduce_fusion.11
  70.6 69.0 %all-gather.9.cloned.1.call-done = bf16[1,256,7168]{1,2,0:T(8,128)(2,1)} async-done(((bf16[1,256,448]{1,2,0:T(8,128)(2,1)}), bf16[1,256,7168]{1,2,0:T(8,128)(2,1)}) %all-gather.9.cloned.1.call-update) | async-done | bytes 3670032 | tf_op jit(solution)/shard_map/all_gather | solution.py:63
  139.7 2.9 multiply_reduce_fusion.3
  142.8 3.7 fusion.45
  151.6 4.2 fusion.8
  155.8 80.2 %all-gather.11.cloned.1.call-done = bf16[1,7168,256]{2,1,0:T(8,128)(2,1)} async-done(((bf16[1,448,256]{2,1,0:T(8,128)(2,1)}), bf16[1,7168,256]{2,1,0:T(8,128)(2,1)}) %all-gather.11.cloned.1.call-update) | async-done | bytes 3670032 | tf_op jit(solution)/shard_map/all_gather | solution.py:64
  236.0 3.5 multiply_reduce_fusion.7
  239.6 2.9 multiply_reduce_fusion.1
  242.7 3.8 fusion.41
  247.7 2.7 collective-permute-start.15
  253.8 2.8 fusion.17
  256.5 33.4 %collective-permute-done.15 = bf16[128,7168]{1,0:T(8,128)(2,1)S(1)} collective-permute-done((bf16[128,7168]{1,0:T(8,128)(2,1)S(1)}, bf16[128,7168]{1,0:T(8,128)(2,1)S(1)}, u32[]{:S(2)}, u32[]{:S(2)}) %collective-permute-start.15) | collective-permute-done | bytes 1835040 | tf_op jit(solution)/shard_map/ppermute | solution.py:16
  292.4 3.7 pad_maximum_fusion.1
  296.0 18.5 %copy.23 = bf16[2,256,7168]{1,0,2:T(2,128)(2,1)} copy(bf16[2,256,7168]{2,1,0:T(8,128)(2,1)} %pad_maximum_fusion.1) | data formatting | bytes 14680064 | tf_op jit(solution)/shard_map/stack | solution.py:93
  314.8 3.5 multiply_reduce_fusion.2
  318.5 5.4 fusion.43
  325.2 3.3 fusion.19
  328.5 2.9 multiply_reduce_fusion
  331.7 3.4 fusion.39
  336.9 2.9 fusion.7
  339.8 3.2 fusion.18
  343.1 6.8 pad_maximum_fusion
  352.2 3.5 multiply_reduce_fusion.15
  359.0 5.8 collective-permute-start
  368.0 3.5 multiply_reduce_fusion.13
  371.6 4.7 fusion.22
  377.6 101.6 %collective-permute-done = bf16[128,7168]{1,0:T(8,128)(2,1)} collective-permute-done((bf16[128,7168]{1,0:T(8,128)(2,1)}, bf16[128,7168]{1,0:T(8,128)(2,1)}, u32[]{:S(2)}, u32[]{:S(2)}) %collective-permute-start) | collective-permute-done | bytes 1835040 | tf_op jit(solution)/shard_map/ppermute | solution.py:16
  483.8 4.2 fusion.29
  488.0 3.9 fusion.99
  494.7 3.4 multiply_reduce_fusion.12
  498.2 5.0 fusion.98
  503.2 68.8 %all-reduce.3.cloned.1.call-done = bf16[2,256,7168]{1,0,2:T(2,128)(2,1)} async-done(((bf16[2,256,7168]{1,0,2:T(2,128)(2,1)}), bf16[2,256,7168]{1,0,2:T(2,128)(2,1)}) %all-reduce.3.cloned.1.call-update) | async-done | bytes 7340048
  574.0 73.5 %reduce-scatter.10.cloned.1.call-done = bf16[448,2]{1,0:T(8,128)(2,1)} async-done(((bf16[7168,2]{1,0:T(8,128)(2,1)}), bf16[448,2]{1,0:T(8,128)(2,1)}) %reduce-scatter.10.cloned.1.call-update) | async-done | bytes 1808
  651.1 94.4 %reduce-scatter.8.cloned.1.call-done = bf16[2,448,256]{2,1,0:T(8,128)(2,1)} async-done(((bf16[2,7168,256]{2,1,0:T(8,128)(2,1)}), bf16[2,448,256]{2,1,0:T(8,128)(2,1)}) %reduce-scatter.8.cloned.1.call-update) | async-done | bytes 458768 | tf_op jit(solution)/shard_map/reduce_scatter | solution.py:96
  747.4 5.2 fusion.28
  754.1 55.9 %reduce-scatter.12.cloned.1.call-done = bf16[16,2]{1,0:T(8,128)(2,1)} async-done(((bf16[256,2]{1,0:T(8,128)(2,1)}), bf16[16,2]{1,0:T(8,128)(2,1)}) %reduce-scatter.12.cloned.1.call-update) | async-done | bytes 80
  811.9 2.7 collective-permute-done.22
  818.1 3.0 collective-permute-start.24
  821.6 3.0 collective-permute-start.27
  826.8 7.4 collective-permute-done.20
  836.4 5.3 collective-permute-done.21
  (179 shorter events, 78.6 us)
Async XLA Ops:
  7.2 59.9 %all-gather.7.cloned.1.call-start = ((), (), s32[]{:S(2)}) async-start(), calls=%async_computation.5 | async-start | bytes 3899392 | tf_op jit(solution)/shard_map/all_gather | solution.py:62
  7.9 131.7 %all-gather.9.cloned.1.call-start = ((), (), s32[]{:S(2)}) async-start(), calls=%async_computation.6 | async-start | bytes 3899392 | tf_op jit(solution)/shard_map/all_gather | solution.py:63
  8.7 227.4 %all-gather.11.cloned.1.call-start = ((), (), s32[]{:S(2)}) async-start(), calls=%async_computation.7 | async-start | bytes 3899392 | tf_op jit(solution)/shard_map/all_gather | solution.py:64
  8.7 7.9 collective-permute-start.4
  16.6 6.8 collective-permute-start.5
  23.4 7.5 collective-permute-start.6
  31.6 7.0 collective-permute-start.10
  33.9 8.9 %collective-permute-start.1 = (bf16[1,7168]{1,0:T(2,128)(2,1)S(1)}, bf16[1,7168]{1,0:T(2,128)(2,1)S(1)}, u32[]{:S(2)}, u32[]{:S(2)}) collective-permute-start(bf16[1,7168]{1,0:T(2,128)(2,1)S(1)} %convert_element_type.345), channel_id=1, source_target_pairs={{0,16},{16,0},{32,48},{48,32},{64,80},{80,64},{96,112},{112,96},{1... | collective-permute-start | bytes 43016 | tf_op jit(solution)/shard_map/ppermute | solution.py:10
  35.2 7.0 collective-permute-start.7
  38.6 6.6 collective-permute-start.11
  42.2 7.3 collective-permute-start.8
  42.8 6.9 collective-permute-start.2
  45.3 9.8 %collective-permute-start.12 = (bf16[1,256,448]{1,2,0:T(8,128)(2,1)S(1)}, bf16[1,256,448]{1,2,0:T(8,128)(2,1)S(1)}, u32[]{:S(2)}, u32[]{:S(2)}) collective-permute-start(bf16[1,256,448]{1,2,0:T(8,128)(2,1)S(1)} %collective-permute-done.11), channel_id=1, source_target_pairs={{0,64},{16,80},{32,96},{48,112},{64,0},{80,16},{96,32},{112,48},{1... | collective-permute-start | bytes 688136 | tf_op jit(solution)/shard_map/ppermute | solution.py:10
  49.6 5.1 collective-permute-start.9
  49.6 5.4 collective-permute-start.3
  57.3 9.8 %copy-start.15 = (f32[1,7168]{1,0:T(1,128)S(1)}, f32[1,7168]{1,0:T(1,128)}, u32[]{:S(2)}) copy-start(f32[1,7168]{1,0:T(1,128)} %param.16) | copy-start | bytes 86020
  57.3 182.2 %all-to-all-start = ((bf16[16,256,448]{1,2,0:T(8,128)(2,1)}), bf16[16,256,448]{1,2,0:T(8,128)(2,1)}, u32[]{:S(2)}, u32[]{:S(2)}) async-start(bf16[16,256,448]{1,2,0:T(8,128)(2,1)} %stack.31), calls=%async_computation | async-start | bytes 7340032 | tf_op jit(solution)/shard_map/all_to_all | solution.py:59
  65.4 506.6 %all-reduce.3.cloned.1.call-start = ((), (), s32[]{:S(2)}) async-start(), calls=%async_computation.10 | async-start | bytes 14680064
  67.1 72.6 %copy-start.8 = (bf16[1,128,7168]{2,1,0:T(8,128)(2,1)S(1)}, bf16[1,128,7168]{2,1,0:T(8,128)(2,1)}, u32[]{:S(2)}) copy-start(bf16[1,128,7168]{2,1,0:T(8,128)(2,1)} %param.12) | copy-start | bytes 5505028
  67.1 72.6 %copy-start.18 = (f32[1,256]{1,0:T(1,128)S(1)}, f32[1,256]{1,0:T(1,128)}, u32[]{:S(2)}) copy-start(f32[1,256]{1,0:T(1,128)} %param.18) | copy-start | bytes 3076
  146.6 4.3 copy-start.19
  149.0 103.4 %collective-permute-start.14 = (bf16[128,7168]{1,0:T(8,128)(2,1)}, bf16[128,7168]{1,0:T(8,128)(2,1)}, u32[]{:S(2)}, u32[]{:S(2)}) collective-permute-start(bf16[128,7168]{1,0:T(8,128)(2,1)} %fusion.52), channel_id=1, source_target_pairs={{16,0},{32,16},{48,32},{64,48},{80,64},{96,80},{112,96},{17,1},{33... | collective-permute-start | bytes 5505032 | tf_op jit(solution)/shard_map/ppermute | solution.py:16
  246.5 3.9 copy-start.21
  247.7 42.2 %collective-permute-start.15 = (bf16[128,7168]{1,0:T(8,128)(2,1)S(1)}, bf16[128,7168]{1,0:T(8,128)(2,1)S(1)}, u32[]{:S(2)}, u32[]{:S(2)}) collective-permute-start(bf16[128,7168]{1,0:T(8,128)(2,1)S(1)} %fusion.54), channel_id=1, source_target_pairs={{0,16},{16,32},{32,48},{48,64},{64,80},{80,96},{96,112},{1,17},{17... | collective-permute-start | bytes 5505032 | tf_op jit(solution)/shard_map/ppermute | solution.py:16
  314.6 333.0 %reduce-scatter.10.cloned.1.call-start = ((), (), s32[]{:S(2)}) async-start(), calls=%async_computation.8 | async-start | bytes 1949696
  325.2 6.3 copy-start.22
  343.1 402.4 %reduce-scatter.8.cloned.1.call-start = ((), (), s32[]{:S(2)}) async-start(), calls=%async_computation.4 | async-start | bytes 7798784 | tf_op jit(solution)/shard_map/reduce_scatter | solution.py:96
  349.9 460.1 %reduce-scatter.12.cloned.1.call-start = ((), (), s32[]{:S(2)}) async-start(), calls=%async_computation.9 | async-start | bytes 69632
  352.2 4.3 copy-start.12
  356.5 8.3 copy-start.23
  359.0 120.2 %collective-permute-start = (bf16[128,7168]{1,0:T(8,128)(2,1)}, bf16[128,7168]{1,0:T(8,128)(2,1)}, u32[]{:S(2)}, u32[]{:S(2)}) collective-permute-start(bf16[128,7168]{1,0:T(8,128)(2,1)} %fusion.20), channel_id=1, source_target_pairs={{0,16},{16,32},{32,48},{48,64},{64,80},{80,96},{96,112},{1,17},{17... | collective-permute-start | bytes 5505032 | tf_op jit(solution)/shard_map/ppermute | solution.py:16
  371.6 109.6 %copy-start.20 = (bf16[1,7168,256]{2,1,0:T(8,128)(2,1)S(1)}, bf16[1,7168,256]{2,1,0:T(8,128)(2,1)}, u32[]{:S(2)}) copy-start(bf16[1,7168,256]{2,1,0:T(8,128)(2,1)} %all-gather.7.cloned.1.call-done) | copy-start | bytes 11010052
  376.3 116.4 %collective-permute-start.13 = (bf16[128,7168]{1,0:T(8,128)(2,1)}, bf16[128,7168]{1,0:T(8,128)(2,1)}, u32[]{:S(2)}, u32[]{:S(2)}) collective-permute-start(bf16[128,7168]{1,0:T(8,128)(2,1)} %fusion.22), channel_id=1, source_target_pairs={{16,0},{32,16},{48,32},{64,48},{80,64},{96,80},{112,96},{17,1},{33... | collective-permute-start | bytes 5505032 | tf_op jit(solution)/shard_map/ppermute | solution.py:16
  483.8 4.2 copy-start.4
  483.8 4.2 copy-start.14
  573.9 75.7 %collective-permute-start.25 = (bf16[256,448]{0,1:T(8,128)(2,1)S(1)}, bf16[256,448]{0,1:T(8,128)(2,1)S(1)}, u32[]{:S(2)}, u32[]{:S(2)}) collective-permute-start(bf16[256,448]{0,1:T(8,128)(2,1)S(1)} %bitcast.248), channel_id=1, source_target_pairs={{0,16},{16,0},{32,48},{48,32},{64,80},{80,64},{96,112},{112,96},{1... | collective-permute-start | bytes 688136 | tf_op jit(solution)/shard_map/ppermute | solution.py:10
  648.7 103.9 %collective-permute-start.16 = (bf16[448]{0:T(512)(128)(2,1)S(1)}, bf16[448]{0:T(512)(128)(2,1)S(1)}, u32[]{:S(2)}, u32[]{:S(2)}) collective-permute-start(bf16[448]{0:T(512)(128)(2,1)S(1)} %get-tuple-element.44), channel_id=1, source_target_pairs={{0,16},{16,0},{32,48},{48,32},{64,80},{80,64},{96,112},{112,96},{1... | collective-permute-start | bytes 2696 | tf_op jit(solution)/shard_map/ppermute | solution.py:10
  649.6 172.0 %collective-permute-start.26 = (bf16[256,448]{0,1:T(8,128)(2,1)S(1)}, bf16[256,448]{0,1:T(8,128)(2,1)S(1)}, u32[]{:S(2)}, u32[]{:S(2)}) collective-permute-start(bf16[256,448]{0,1:T(8,128)(2,1)S(1)} %collective-permute-done.25), channel_id=1, source_target_pairs={{0,32},{16,48},{32,0},{48,16},{64,96},{80,112},{96,64},{112,80},{1... | collective-permute-start | bytes 688136 | tf_op jit(solution)/shard_map/ppermute | solution.py:10
  746.5 78.2 %collective-permute-start.19 = (bf16[448,256]{1,0:T(8,128)(2,1)S(1)}, bf16[448,256]{1,0:T(8,128)(2,1)S(1)}, u32[]{:S(2)}, u32[]{:S(2)}) collective-permute-start(bf16[448,256]{1,0:T(8,128)(2,1)S(1)} %slice_bitcast_fusion), channel_id=1, source_target_pairs={{0,16},{16,0},{32,48},{48,32},{64,80},{80,64},{96,112},{112,96},{1... | collective-permute-start | bytes 688136 | tf_op jit(solution)/shard_map/ppermute | solution.py:10
  747.4 94.3 %copy-start.16 = (bf16[2,448,256]{2,1,0:T(8,128)(2,1)S(1)}, bf16[2,448,256]{2,1,0:T(8,128)(2,1)}, u32[]{:S(2)}) copy-start(bf16[2,448,256]{2,1,0:T(8,128)(2,1)} %reduce-scatter.8.cloned.1.call-done) | copy-start | bytes 1376260
  752.7 68.5 %collective-permute-start.17 = (bf16[448]{0:T(512)(128)(2,1)S(1)}, bf16[448]{0:T(512)(128)(2,1)S(1)}, u32[]{:S(2)}, u32[]{:S(2)}) collective-permute-start(bf16[448]{0:T(512)(128)(2,1)S(1)} %collective-permute-done.16), channel_id=1, source_target_pairs={{0,32},{16,48},{32,0},{48,16},{64,96},{80,112},{96,64},{112,80},{1... | collective-permute-start | bytes 2696 | tf_op jit(solution)/shard_map/ppermute | solution.py:10
  811.0 3.5 collective-permute-start.22
  814.6 3.5 collective-permute-start.23
  818.1 7.2 collective-permute-start.24
  821.1 5.1 collective-permute-start.18
  821.6 14.0 %collective-permute-start.27 = (bf16[256,448]{0,1:T(8,128)(2,1)S(1)}, bf16[256,448]{0,1:T(8,128)(2,1)S(1)}, u32[]{:S(2)}, u32[]{:S(2)}) collective-permute-start(bf16[256,448]{0,1:T(8,128)(2,1)S(1)} %collective-permute-done.26), channel_id=1, source_target_pairs={{0,64},{16,80},{32,96},{48,112},{64,0},{80,16},{96,32},{112,48},{1... | collective-permute-start | bytes 688136 | tf_op jit(solution)/shard_map/ppermute | solution.py:10
  824.7 9.5 %collective-permute-start.20 = (bf16[448,256]{1,0:T(8,128)(2,1)S(1)}, bf16[448,256]{1,0:T(8,128)(2,1)S(1)}, u32[]{:S(2)}, u32[]{:S(2)}) collective-permute-start(bf16[448,256]{1,0:T(8,128)(2,1)S(1)} %collective-permute-done.19), channel_id=1, source_target_pairs={{0,32},{16,48},{32,0},{48,16},{64,96},{80,112},{96,64},{112,80},{1... | collective-permute-start | bytes 688136 | tf_op jit(solution)/shard_map/ppermute | solution.py:10
  834.2 7.5 collective-permute-start.21
  (14 other events, 39.5 us)
Sparse Core Ops, SparseCore 0:
  10.4 56.6 all-gather.6
  69.5 70.1 all-gather.8
  142.6 93.3 all-gather.10
  314.7 257.2 all-reduce.2
  575.8 71.7 reduce-scatter.9
  652.2 93.2 reduce-scatter.7
  749.6 60.3 reduce-scatter.11
